TPU v7x, 32 devices: a whole 2x2x4 slice. The times are simulated.
32 devices in a mesh: lat: 8 (over y, x, core), lon: 4 (over z).
Axes of the slice: x: 2, y: 2, z: 4, core: 2. Of those that a mesh axis runs over, the one named last changes fastest.
Arguments:
- prediction_deviation: bfloat16 [16, 256, 128, 80], P(None, 'lat', 'lon'), may hold values from -6 to 6
- humid_energy_misfit: float32 [16, 256, 128], P(None, 'lat', 'lon'), may hold values from -0.6 to 0.6
- sensor_space_deviation: bfloat16 [8, 4, 80, 1024], P('lat', 'lon'), may hold values from -6 to 6
- scaled_departure: float32 [8, 4, 1024], P('lat', 'lon'), may hold values from -6 to 6
- datum_location: int32 [8, 4, 2, 1024], P('lat', 'lon'), may hold values from 0 to 31, as said below
- taper_category: int32 [8, 4, 1024], P('lat', 'lon'), may hold values from 0 to 3
- datum_patch_codes: int32 [8, 4, 4, 1024], P('lat', 'lon'), may hold values from -1 to 8, as said below
- active_datum_tally: int32 [8, 4], P('lat', 'lon'), may hold values from 128 to 1024, as said below
Outputs:
- impact: float32 [8, 4, 1024], P('lat', 'lon')
Inputs may be any that keep to these rules, and one draw needn't show every extreme that they name: `datum_location`: row and column of the observation's cell, each from 0 to 31. `datum_patch_codes`: codes are 3 (dr + 1) + (ds + 1) for a tile offset (dr, ds) from the owner, or -1 for an empty entry. Entry 0 is always 4, the owner; the named codes of a slot are distinct and never name a tile beyond the first or last tile row. At least 128 live slots on every tile, and 1024 on some tile in every draw; slots from active_datum_tally on carry no observation.
All inputs are finite; a program needn't handle non-finite values.
Results may differ from a plain program's by a relative error of at most 0.0055.
Values may be sent and summed in bfloat16 or wider, within the bound.
A program may use at most 64 MiB of HBM per device.

v0:
```python
import jax
import jax.numpy as jnp
from jax import lax
from jax.sharding import PartitionSpec as P


def padded(block, sides, width):
    for axis, dim in sides:
        count = lax.axis_size(axis)
        forward = [(i, i + 1) for i in range(count - 1)]
        forward.append((count - 1, 0))
        backward = [(target, source) for source, target in forward]
        low = lax.ppermute(
            lax.slice_in_dim(block, block.shape[dim] - width, None, axis=dim), axis, forward
        )
        high = lax.ppermute(lax.slice_in_dim(block, 0, width, axis=dim), axis, backward)
        block = jnp.concatenate([low, block, high], axis=dim)
    return block


def taper_weights(obs_row, obs_col, obs_class, cell_rows, cell_cols, allowed, patch_span_points):
    radius = patch_span_points * (1.0 + obs_class) * 0.125
    radius_sq = (radius * radius)[:, None]
    distance = (cell_rows[None, :] - obs_row[:, None]) ** 2 + (
        cell_cols[None, :] - obs_col[:, None]
    ) ** 2
    fraction = 1.0 - distance / radius_sq
    return jnp.where(allowed & (distance < radius_sq), fraction * fraction, 0.0).astype(
        jnp.bfloat16
    )


def tile_offset(shifted, patch_span_points):
    return (shifted >= patch_span_points).astype(jnp.int32) - (shifted < 0).astype(jnp.int32)


def on_device(
    prediction_deviation,
    humid_energy_misfit,
    sensor_space_deviation,
    scaled_departure,
    datum_location,
    taper_category,
    datum_patch_codes,
    active_datum_tally,
):
    patch_span_points = prediction_deviation.shape[1]
    perturbed_runs = prediction_deviation.shape[3]
    slot_count = sensor_space_deviation.shape[3]
    projected = jnp.sum(
        prediction_deviation.astype(jnp.float32) * humid_energy_misfit[..., None], axis=0
    ).astype(jnp.bfloat16)
    margin = patch_span_points // 2
    window_width = 2 * patch_span_points
    window = padded(projected, (("lat", 0), ("lon", 1)), margin)
    offsets = jnp.arange(window_width, dtype=jnp.int32) - margin
    cover_codes = datum_patch_codes[0, 0]
    position = datum_location[0, 0].astype(jnp.float32)
    taper_size = taper_category[0, 0].astype(jnp.float32)
    block_rows = patch_span_points // 2
    projection = jnp.zeros((slot_count, perturbed_runs), jnp.float32)
    for quarter in range(4):
        row_offsets = offsets[quarter * block_rows : (quarter + 1) * block_rows]
        rel_rows = jnp.repeat(row_offsets, window_width)
        rel_cols = jnp.tile(offsets, block_rows)
        tile_code = (
            3 * (tile_offset(rel_rows, patch_span_points) + 1)
            + tile_offset(rel_cols, patch_span_points)
            + 1
        )
        allowed = jnp.any(cover_codes[:, :, None] == tile_code[None, None, :], axis=0)
        weights = taper_weights(
            position[0],
            position[1],
            taper_size,
            rel_rows.astype(jnp.float32),
            rel_cols.astype(jnp.float32),
            allowed,
            patch_span_points,
        )
        window_block = window[quarter * block_rows : (quarter + 1) * block_rows].reshape(
            -1, perturbed_runs
        )
        projection = projection + jnp.dot(weights, window_block, preferred_element_type=jnp.float32)
    summed = jnp.sum(projection * sensor_space_deviation[0, 0].T.astype(jnp.float32), axis=1)
    live_slots = (jnp.arange(slot_count, dtype=jnp.int32) < active_datum_tally[0, 0]).astype(
        jnp.float32
    )
    impact = scaled_departure[0, 0] * summed / (perturbed_runs - 1) * live_slots
    return impact[None, None]


def solution(mesh):
    return jax.shard_map(
        on_device,
        mesh=mesh,
        in_specs=(
            P(None, "lat", "lon", None),
            P(None, "lat", "lon"),
            P("lat", "lon", None, None),
            P("lat", "lon", None),
            P("lat", "lon", None, None),
            P("lat", "lon", None),
            P("lat", "lon", None, None),
            P("lat", "lon"),
        ),
        out_specs=P("lat", "lon", None),
        check_vma=False,
    )
```

profile of v0, /device:TPU:0, one launch (start us, length us, event | category | flops | bytes accessed | tf_op | source)
XLA Modules:
  0.0 59.2 jit_solution(7190022967902292667)
XLA Ops:
  0.0 4.5 %multiply_reduce_fusion = bf16[32,32,80]{2,1,0:T(8,128)(2,1)S(1)} fusion(bf16[16,32,32,80]{3,2,1,0:T(8,128)(2,1)} %param.8, f32[16,32,32]{2,1,0:T(8,128)} %param.9), kind=kLoop, calls=%fused_computation.4 | loop fusion | flops 3850240 | bytes 2850816 | tf_op jit(solution)/shard_map/reduce_sum | solution.py:50
  4.5 0.7 %fusion.42 = (bf16[16,32,80]{2,1,0:T(8,128)(2,1)}, bf16[16,32,80]{2,1,0:T(8,128)(2,1)}) fusion(bf16[32,32,80]{2,1,0:T(8,128)(2,1)S(1)} %multiply_reduce_fusion), kind=kLoop, calls=%fused_computation.79 | loop fusion | bytes 327680 | tf_op jit(solution)/shard_map/slice | solution.py:14
  5.2 3.4 %collective-permute-start.1 = (bf16[16,32,80]{2,1,0:T(8,128)(2,1)}, bf16[16,32,80]{2,1,0:T(8,128)(2,1)S(1)}, u32[]{:S(2)}, u32[]{:S(2)}) collective-permute-start(bf16[16,32,80]{2,1,0:T(8,128)(2,1)} %get-tuple-element.16), channel_id=1, source_target_pairs={{4,0},{8,4},{12,8},{16,12},{20,16},{24,20},{28,24},{0,28},{5,1},{9... | collective-permute-start | bytes 245768 | tf_op jit(solution)/shard_map/ppermute | solution.py:16
  8.6 0.7 %slice_convert_fusion = (f32[16]{0:T(128)}, f32[16]{0:T(128)}, s32[16]{0:T(128)S(1)}, s32[16]{0:T(128)S(1)}, f32[16]{0:T(128)}, /*index=5*/s32[16]{0:T(128)S(1)}, f32[16]{0:T(128)S(1)}, s32[16]{0:T(128)S(1)}) fusion(s32[64]{0:T(128)S(1)} %iota_add_fusion), kind=kLoop, calls=%fused_computation.64 | loop fusion | flops 512 | bytes 768 | tf_op jit(solution)/shard_map/convert_element_type | solution.py:76
  9.3 0.7 %reshape.241 = s32[1024]{0:T(1024)} reshape(s32[16,64]{1,0:T(8,128)S(1)} %get-tuple-element.30) | data formatting | bytes 8192 | tf_op jit(solution)/shard_map/add | solution.py:67
  10.0 0.7 %reshape.237 = s32[1024]{0:T(1024)} reshape(s32[16,64]{1,0:T(8,128)S(1)} %get-tuple-element.28) | data formatting | bytes 8192 | tf_op jit(solution)/shard_map/add | solution.py:67
  10.6 0.7 %reshape.239 = s32[1024]{0:T(1024)} reshape(s32[16,64]{1,0:T(8,128)S(1)} %get-tuple-element.29) | data formatting | bytes 8192 | tf_op jit(solution)/shard_map/add | solution.py:67
  12.0 0.7 %convert_element_type.240 = f32[1024]{0:T(1024)} reshape(f32[16,64]{1,0:T(8,128)S(1)} %broadcast_in_dim.49) | data formatting | bytes 8192 | tf_op jit(solution)/shard_map/convert_element_type | solution.py:76
  13.3 13.2 %compare_reduce_fusion = (pred[1024,1024]{1,0:T(8,128)(4,1)S(1)}, pred[1024,1024]{1,0:T(8,128)(4,1)}, pred[1024,1024]{1,0:T(8,128)(4,1)S(1)}, pred[1024,1024]{1,0:T(8,128)(4,1)S(1)}) fusion(s32[1024]{0:T(1024)} %reshape.241, s32[4,1024]{1,0:T(4,128)S(1)} %bitcast.26, s32[1024]{0:T(1024)} %reshape.237, s32[1024]{0:T(1024)} %reshape.239, s32[1024]{0:T(1024)} %reshape.235), kind=kLoop, calls=%fused_computation | loop fusion | flops 29360128 | bytes 4227072 | tf_op jit(solution)/shard_map/reduce_or | solution.py:71
  26.6 0.8 %broadcast_in_dim.46 = f32[16,64]{1,0:T(8,128)S(1)} broadcast(f32[16]{0:T(128)} %get-tuple-element.23), dimensions={0} | broadcast | bytes 4160 | tf_op jit(solution)/shard_map/broadcast_in_dim | solution.py:64
  27.3 0.7 %convert_element_type.229 = f32[1024]{0:T(1024)} reshape(f32[16,64]{1,0:T(8,128)S(1)} %broadcast_in_dim.46) | data formatting | bytes 8192 | tf_op jit(solution)/shard_map/convert_element_type | solution.py:76
  28.6 0.7 %convert_element_type.245 = f32[1024]{0:T(1024)} reshape(f32[16,64]{1,0:T(8,128)S(1)} %broadcast_in_dim.51) | data formatting | bytes 8192 | tf_op jit(solution)/shard_map/convert_element_type | solution.py:76
  29.3 0.7 %broadcast_in_dim.53 = f32[16,64]{1,0:T(8,128)S(1)} broadcast(f32[16]{0:T(128)} %get-tuple-element.19), dimensions={0} | broadcast | bytes 4160 | tf_op jit(solution)/shard_map/broadcast_in_dim | solution.py:64
  30.0 0.7 %convert_element_type.250 = f32[1024]{0:T(1024)} reshape(f32[16,64]{1,0:T(8,128)S(1)} %broadcast_in_dim.53) | data formatting | bytes 8192 | tf_op jit(solution)/shard_map/convert_element_type | solution.py:76
  31.4 1.0 %pad_maximum_fusion.1 = bf16[64,32,80]{2,1,0:T(8,128)(2,1)S(1)} fusion(bf16[16,32,80]{2,1,0:T(8,128)(2,1)S(1)} %collective-permute-done.1, bf16[32,32,80]{2,1,0:T(8,128)(2,1)S(1)} %multiply_reduce_fusion, bf16[16,32,80]{2,1,0:T(8,128)(2,1)} %collective-permute-done), kind=kLoop, calls=%fused_computation.32 | loop fusion | flops 327680 | bytes 655360 | tf_op jit(solution)/shard_map/concatenate | solution.py:17
  32.5 3.7 %collective-permute-start.3 = (bf16[64,16,80]{2,1,0:T(8,128)(2,1)S(1)}, bf16[64,16,80]{2,1,0:T(8,128)(2,1)S(1)}, u32[]{:S(2)}, u32[]{:S(2)}) collective-permute-start(bf16[64,16,80]{2,1,0:T(8,128)(2,1)S(1)} %get-tuple-element.14), channel_id=1, source_target_pairs={{1,0},{2,1},{3,2},{0,3},{5,4},{6,5},{7,6},{4,7},{9,8},{10,9},{11,1... | collective-permute-start | bytes 491528 | tf_op jit(solution)/shard_map/ppermute | solution.py:16
  36.2 0.7 %multiply_multiply_fusion = f32[1,1,1024]{2,1,0:T(1,128)S(1)} fusion(s32[1,1,1024]{2,1,0:T(1,128)} %param.13), kind=kLoop, calls=%fused_computation.39 | loop fusion | flops 4096 | bytes 8192 | tf_op jit(solution)/shard_map/mul | solution.py:23
  36.9 6.0 %collective-permute-done.3 = bf16[64,16,80]{2,1,0:T(8,128)(2,1)S(1)} collective-permute-done((bf16[64,16,80]{2,1,0:T(8,128)(2,1)S(1)}, bf16[64,16,80]{2,1,0:T(8,128)(2,1)S(1)}, u32[]{:S(2)}, u32[]{:S(2)}) %collective-permute-start.3) | collective-permute-done | bytes 163872 | tf_op jit(solution)/shard_map/ppermute | solution.py:16
  42.9 5.3 %collective-permute-done.2 = bf16[64,16,80]{2,1,0:T(8,128)(2,1)S(1)} collective-permute-done((bf16[64,16,80]{2,1,0:T(8,128)(2,1)S(1)}, bf16[64,16,80]{2,1,0:T(8,128)(2,1)S(1)}, u32[]{:S(2)}, u32[]{:S(2)}) %collective-permute-start.2) | collective-permute-done | bytes 163872 | tf_op jit(solution)/shard_map/ppermute | solution.py:13
  48.1 1.2 %pad_maximum_fusion = bf16[64,64,80]{2,1,0:T(8,128)(2,1)S(1)} fusion(bf16[64,16,80]{2,1,0:T(8,128)(2,1)S(1)} %collective-permute-done.3, bf16[16,32,80]{2,1,0:T(8,128)(2,1)S(1)} %collective-permute-done.1, bf16[32,32,80]{2,1,0:T(8,128)(2,1)S(1)} %multiply_reduce_fusion, bf16[16,32,80]{2,1,0:T(8,128)(2,1)} %collective-permute-done, ...), kind=kLoop, calls=%fused_computation.31 | loop fusion | flops 3276800 | bytes 1310720 | tf_op jit(solution)/shard_map/concatenate | solution.py:17
  49.5 2.2 %fusion.10 = f32[1024,80]{0,1:T(8,128)S(1)} fusion(bf16[1024,80]{1,0:T(8,128)(2,1)S(1)} %bitcast.25, pred[1024,1024]{1,0:T(8,128)(4,1)S(1)} %copy-done, f32[1024]{0:T(1024)S(1)} %copy-done.4, f32[1024]{0:T(1024)S(1)} %bitcast.28, f32[1024]{0:T(1024)S(1)} %bitcast.36, f32[1024]{0:T(1024)S(1)} %convert_element_type.232, f32[1024]{0:T(1024)S(1)} %bitcast.32), kind=kOutput, calls=%fused_computation.23 | convolution fusion | flops 180355072 | bytes 1560576 | tf_op jit(solution)/shard_map/dot_general | solution.py:84
  51.7 2.2 %fusion.16 = f32[1024,80]{0,1:T(8,128)S(1)} fusion(f32[1024,80]{0,1:T(8,128)S(1)} %fusion.10, bf16[1024,80]{1,0:T(8,128)(2,1)S(1)} %bitcast.24, pred[1024,1024]{1,0:T(8,128)(4,1)S(1)} %get-tuple-element.8, f32[1024]{0:T(1024)S(1)} %bitcast.29, f32[1024]{0:T(1024)S(1)} %bitcast.37, f32[1024]{0:T(1024)S(1)} %convert_element_type.232, f32[1024]{0:T(1024)S(1)} %bitcast.33, ...), kind=kOutput, calls=%fused_computation.29 | convolution fusion | flops 180436992 | bytes 1888256 | tf_op jit(solution)/shard_map/dot_general | solution.py:84
  53.9 2.2 %fusion.15 = f32[1024,80]{0,1:T(8,128)S(1)} fusion(f32[1024,80]{0,1:T(8,128)S(1)} %fusion.16, bf16[1024,80]{1,0:T(8,128)(2,1)S(1)} %bitcast.23, pred[1024,1024]{1,0:T(8,128)(4,1)S(1)} %get-tuple-element.7, f32[1024]{0:T(1024)S(1)} %copy-done.6, f32[1024]{0:T(1024)S(1)} %bitcast.30, f32[1024]{0:T(1024)S(1)} %bitcast.38, f32[1024]{0:T(1024)S(1)} %convert_element_type.232, ...), kind=kOutput, calls=%fused_computation.28 | convolution fusion | flops 180436992 | bytes 1888256 | tf_op jit(solution)/shard_map/dot_general | solution.py:84
  56.1 2.5 %fusion.17 = f32[1024]{0:T(1024)S(1)} fusion(f32[1024,80]{0,1:T(8,128)S(1)} %fusion.15, bf16[1024,80]{1,0:T(8,128)(2,1)S(1)} %bitcast.22, pred[1024,1024]{1,0:T(8,128)(4,1)S(1)} %get-tuple-element.5, f32[1024]{0:T(1024)S(1)} %copy-done.5, f32[1024]{0:T(1024)S(1)} %bitcast.31, f32[1024]{0:T(1024)S(1)} %bitcast.39, f32[1024]{0:T(1024)S(1)} %convert_element_type.232, ...), kind=kOutput, calls=%fused_computation.30 | convolution fusion | flops 180681728 | bytes 1728512 | tf_op jit(solution)/shard_map/dot_general | solution.py:84
  (40 shorter events, 2.9 us)
Async XLA Ops:
  0.0 12.7 %copy-start.2 = (s32[1,1,2,1024]{3,2,1,0:T(2,128)S(1)}, s32[1,1,2,1024]{3,2,1,0:T(2,128)}, u32[]{:S(2)}) copy-start(s32[1,1,2,1024]{3,2,1,0:T(2,128)} %param.12) | copy-start | bytes 24580
  0.0 13.3 %copy-start.1 = (s32[1,1,4,1024]{3,2,1,0:T(4,128)S(1)}, s32[1,1,4,1024]{3,2,1,0:T(4,128)}, u32[]{:S(2)}) copy-start(s32[1,1,4,1024]{3,2,1,0:T(4,128)} %param.14) | copy-start | bytes 49156
  5.2 26.2 %collective-permute-start.1 = (bf16[16,32,80]{2,1,0:T(8,128)(2,1)}, bf16[16,32,80]{2,1,0:T(8,128)(2,1)S(1)}, u32[]{:S(2)}, u32[]{:S(2)}) collective-permute-start(bf16[16,32,80]{2,1,0:T(8,128)(2,1)} %get-tuple-element.16), channel_id=1, source_target_pairs={{4,0},{8,4},{12,8},{16,12},{20,16},{24,20},{28,24},{0,28},{5,1},{9... | collective-permute-start | bytes 245768 | tf_op jit(solution)/shard_map/ppermute | solution.py:16
  8.6 22.9 %collective-permute-start = (bf16[16,32,80]{2,1,0:T(8,128)(2,1)}, bf16[16,32,80]{2,1,0:T(8,128)(2,1)}, u32[]{:S(2)}, u32[]{:S(2)}) collective-permute-start(bf16[16,32,80]{2,1,0:T(8,128)(2,1)} %get-tuple-element.15), channel_id=1, source_target_pairs={{0,4},{4,8},{8,12},{12,16},{16,20},{20,24},{24,28},{28,0},{1,5},{5... | collective-permute-start | bytes 245768 | tf_op jit(solution)/shard_map/ppermute | solution.py:13
  26.5 23.0 %copy-start.4 = (f32[1024]{0:T(1024)S(1)}, f32[1024]{0:T(1024)}, u32[]{:S(2)}) copy-start(f32[1024]{0:T(1024)} %convert_element_type.240) | copy-start | bytes 12292
  30.7 18.8 %copy-start = (pred[1024,1024]{1,0:T(8,128)(4,1)S(1)}, pred[1024,1024]{1,0:T(8,128)(4,1)}, u32[]{:S(2)}) copy-start(pred[1024,1024]{1,0:T(8,128)(4,1)} %get-tuple-element.6) | copy-start | bytes 3145732
  30.7 18.8 %copy-start.8 = (f32[1,1,1,1024]{3,2,1,0:T(1,128)S(1)}, f32[1,1,1,1024]{3,2,1,0:T(1,128)}, u32[]{:S(2)}) copy-start(f32[1,1,1,1024]{3,2,1,0:T(1,128)} %get-tuple-element.17) | copy-start | bytes 12292
  30.7 18.8 %copy-start.9 = (f32[1,1,1,1024]{3,2,1,0:T(1,128)S(1)}, f32[1,1,1,1024]{3,2,1,0:T(1,128)}, u32[]{:S(2)}) copy-start(f32[1,1,1,1024]{3,2,1,0:T(1,128)} %get-tuple-element.18) | copy-start | bytes 12292
  32.5 10.4 %collective-permute-start.3 = (bf16[64,16,80]{2,1,0:T(8,128)(2,1)S(1)}, bf16[64,16,80]{2,1,0:T(8,128)(2,1)S(1)}, u32[]{:S(2)}, u32[]{:S(2)}) collective-permute-start(bf16[64,16,80]{2,1,0:T(8,128)(2,1)S(1)} %get-tuple-element.14), channel_id=1, source_target_pairs={{1,0},{2,1},{3,2},{0,3},{5,4},{6,5},{7,6},{4,7},{9,8},{10,9},{11,1... | collective-permute-start | bytes 491528 | tf_op jit(solution)/shard_map/ppermute | solution.py:16
  36.2 12.0 %collective-permute-start.2 = (bf16[64,16,80]{2,1,0:T(8,128)(2,1)S(1)}, bf16[64,16,80]{2,1,0:T(8,128)(2,1)S(1)}, u32[]{:S(2)}, u32[]{:S(2)}) collective-permute-start(bf16[64,16,80]{2,1,0:T(8,128)(2,1)S(1)} %get-tuple-element.13), channel_id=1, source_target_pairs={{0,1},{1,2},{2,3},{3,0},{4,5},{5,6},{6,7},{7,4},{8,9},{9,10},{10,1... | collective-permute-start | bytes 491528 | tf_op jit(solution)/shard_map/ppermute | solution.py:13
  49.5 2.2 %copy-start.7 = (f32[1024]{0:T(1024)S(1)}, f32[1024]{0:T(1024)}, u32[]{:S(2)}) copy-start(f32[1024]{0:T(1024)} %convert_element_type.229) | copy-start | bytes 12292
  51.7 2.2 %copy-start.6 = (f32[1024]{0:T(1024)S(1)}, f32[1024]{0:T(1024)}, u32[]{:S(2)}) copy-start(f32[1024]{0:T(1024)} %convert_element_type.245) | copy-start | bytes 12292
  53.9 2.2 %copy-start.5 = (f32[1024]{0:T(1024)S(1)}, f32[1024]{0:T(1024)}, u32[]{:S(2)}) copy-start(f32[1024]{0:T(1024)} %convert_element_type.250) | copy-start | bytes 12292
  53.9 2.2 %copy-start.10 = (bf16[1,1,80,1024]{3,2,1,0:T(8,128)(2,1)S(1)}, bf16[1,1,80,1024]{3,2,1,0:T(8,128)(2,1)}, u32[]{:S(2)}) copy-start(bf16[1,1,80,1024]{3,2,1,0:T(8,128)(2,1)} %param.10) | copy-start | bytes 491524
  56.1 2.5 %copy-start.3 = (f32[1,1,1024]{2,1,0:T(1,128)S(1)}, f32[1,1,1024]{2,1,0:T(1,128)}, u32[]{:S(2)}) copy-start(f32[1,1,1024]{2,1,0:T(1,128)} %param.11) | copy-start | bytes 12292
where the time goes:
time: 59.5 us; the launch traced here: 59.2 us
  other arithmetic  21.9 us (37%)
  waiting for transfers between devices  11.3 us (19%)
  local copies, waits for them, and re-layouts  9.05 us (15%)
  matrix products  9.01 us (15%)
  starting transfers between devices  7.02 us (12%)
  between operations  0.94 us (2%)
    reduce_or x1, other arithmetic, on_device(): jnp.any(cover_codes[:, :, None] == tile_code[None, None, :], axis=0)  13.2 us
    dot_general x4, matrix products, on_device(): jnp.dot(weights, window_block, preferred_element_type=jnp.float32)  9.01 us
    ppermute x2, starting transfers between devices, padded(): lax.ppermute(lax.slice_in_dim(block, 0, width, axis=dim), axis, backward)  7.02 us
    ppermute x2, waiting for transfers between devices, padded(): lax.ppermute(lax.slice_in_dim(block, 0, width, axis=dim), axis, backward)  6 us
    ppermute x2, waiting for transfers between devices, padded(): lax.ppermute(lax.slice_in_dim(block, block.shape[dim] - width, None, axis...  5.27 us
    reduce_sum x1, other arithmetic, on_device(): jnp.sum(prediction_deviation.astype(jnp.float32) * humid_energy_misfit[.....  4.46 us
    convert_element_type x4, local copies, waits for them, and re-layouts, on_device(): rel_rows.astype(jnp.float32)  2.66 us
    add x4, local copies, waits for them, and re-layouts, on_device(): 3 * (tile_offset(rel_rows, patch_span_points) + 1)  2.64 us
  transfers between devices with their start and end apart: 4, of which 2 were waited for; matrix products, arithmetic and copies ran while one was open for 38% of the time, Pallas kernels for 0%

commit v1 on v0

v1 whole, which is shorter than its diff:
```python
import functools

import jax
import jax.numpy as jnp
from jax import lax
from jax.experimental import pallas as pl
from jax.experimental.pallas import tpu as pltpu
from jax.sharding import PartitionSpec as P

MESH = pl.DeviceIdType.MESH
READ_CHUNKS = 4


def kernel(
    nlat, nlon,
    dev_hbm, mis_hbm, sens_hbm, scaled_hbm, loc_hbm, cat_hbm, codes_hbm, tally_hbm,
    out_ref,
    dev, mis, sens, scaled, loc, cat, codes, tally,
    split, cells, own, halo, bound, taper, acc,
    in_sem, dev_sem, send_sem, recv_sem,
):
    levels, tile, _, members = dev.shape
    half = tile // 2
    slots = sens.shape[1]
    p = lax.axis_index("lat")
    q = lax.axis_index("lon")
    left = lax.rem(q + nlon - 1, nlon)
    right = lax.rem(q + 1, nlon)
    has_up = p > 0
    has_down = p < nlat - 1

    rows_per = tile // READ_CHUNKS
    small = [
        pltpu.make_async_copy(src, dst, in_sem.at[i])
        for i, (src, dst) in enumerate(
            [(mis_hbm, mis), (loc_hbm, loc), (cat_hbm, cat), (codes_hbm, codes),
             (sens_hbm, sens), (scaled_hbm, scaled), (tally_hbm, tally)]
        )
    ]
    reads = [
        pltpu.make_async_copy(
            dev_hbm.at[:, pl.ds(c * rows_per, rows_per)],
            dev.at[:, pl.ds(c * rows_per, rows_per)],
            dev_sem.at[c],
        )
        for c in range(READ_CHUNKS)
    ]
    small[0].start()
    reads[0].start()
    for copy in small[1:4]:
        copy.start()
    for copy in reads[1:]:
        copy.start()
    for copy in small[4:]:
        copy.start()

    barrier = pltpu.get_barrier_semaphore()

    def greet(row):
        for col in (left, q, right):
            pl.semaphore_signal(barrier, inc=1, device_id=(row, col), device_id_type=MESH)

    for col in (left, right):
        pl.semaphore_signal(barrier, inc=1, device_id=(p, col), device_id_type=MESH)
    pl.when(has_up)(lambda: greet(p - 1))
    pl.when(has_down)(lambda: greet(p + 1))

    small[0].wait()
    wide = jnp.concatenate([mis[l] for l in range(levels)], axis=1)
    high = wide.astype(jnp.bfloat16).astype(jnp.float32)
    split[0] = high
    split[1] = wide - high

    for copy in small[1:4]:
        copy.wait()
    place = loc[...].astype(jnp.float32)
    radius = (tile * 0.125) * (1.0 + cat[...].astype(jnp.float32))
    radius_sq = radius * radius
    cover = codes[...]
    barred = [
        jnp.where(jnp.any(cover == code, axis=0, keepdims=True), 0.0, 4.0 * half * half)
        for code in range(9)
    ]
    for j in range(4):
        b = lax.broadcasted_iota(jnp.int32, (half, slots), 0).astype(jnp.float32) + (j - 1) * half
        gap = b - place[1:2]
        gap = gap * gap
        ds = (j + 1) // 2
        for dr in range(3):
            bound[dr * 4 + j] = (gap + barred[3 * dr + ds]).astype(jnp.bfloat16)

    diagonal = (
        lax.rem(lax.broadcasted_iota(jnp.int32, (tile, levels * tile), 1), tile)
        == lax.broadcasted_iota(jnp.int32, (tile, levels * tile), 0)
    )

    peers = 2 + 3 * jnp.minimum(p, 1) + 3 * jnp.minimum(nlat - 1 - p, 1)
    pl.semaphore_wait(barrier, peers)

    def send(yh, xh, kind):
        i = 3 if yh == 0 else 0
        j = 3 if xh == 0 else 0
        row = p - 1 if yh == 0 else p + 1
        col = left if xh == 0 else right
        if kind == "row":
            i, row = yh + 1, p
        if kind == "col":
            j, col = xh + 1, q
        slot = i * 4 + j
        copy = pltpu.make_async_remote_copy(
            src_ref=own.at[2 * yh + xh],
            dst_ref=halo.at[slot],
            send_sem=send_sem.at[slot],
            recv_sem=recv_sem.at[slot],
            device_id=(row, col),
            device_id_type=MESH,
        )
        return slot, copy, kind != "row"

    copies = {}
    for yh in range(2):
        for c in range(yh * READ_CHUNKS // 2, (yh + 1) * READ_CHUNKS // 2):
            reads[c].wait()

        def level_sum(y, _):
            row = yh * half + y
            terms = []
            for s in range(2):
                line = split[s, pl.ds(row, 1), :]
                terms.append(
                    jnp.where(diagonal, jnp.broadcast_to(line, diagonal.shape), 0.0).astype(jnp.bfloat16)
                )
            both = jnp.dot(
                jnp.concatenate(terms, axis=0),
                dev[:, row].reshape(levels * tile, members),
                preferred_element_type=jnp.float32,
            )
            total = both[:tile] + both[tile:]
            cells[0, y] = total[:half]
            cells[1, y] = total[half:]
            return 0

        lax.fori_loop(0, half, level_sum, 0, unroll=4)
        for xh in range(2):
            own[2 * yh + xh] = cells[xh].reshape(half * half, members).T.astype(jnp.bfloat16)
            for kind in ("row", "corner", "col"):
                slot, copy, vertical = send(yh, xh, kind)
                copies[slot] = copy
                if vertical:
                    pl.when(has_up if yh == 0 else has_down)(copy.start)
                else:
                    copy.start()

    row_gap = jnp.broadcast_to(place[0:1], (half, slots)).astype(jnp.bfloat16)
    reach = jnp.broadcast_to(radius_sq, (half, slots)).astype(jnp.bfloat16)
    for i in (1, 2, 0, 3):
        dr = (i + 1) // 2

        def build(y, gap):
            room = reach - gap * gap
            for j in range(4):
                t = jnp.maximum(room - bound[dr * 4 + j], jnp.bfloat16(0))
                taper[i * 4 + j, y] = t * t
            return gap - jnp.bfloat16(1)

        lax.fori_loop(0, half, build, row_gap - jnp.bfloat16((i - 1) * half), unroll=2)

    def product(slot, source):
        return jnp.dot(
            source,
            taper[slot].reshape(half * half, slots),
            preferred_element_type=jnp.float32,
        )

    def add(slot, copy):
        copy.wait_recv()
        acc[...] += product(slot, halo[slot])

    for yh in range(2):
        for xh in range(2):
            value = product((yh + 1) * 4 + xh + 1, own[2 * yh + xh])
            if yh == 0 and xh == 0:
                acc[...] = value
            else:
                acc[...] += value
    for slot in (1, 2, 13, 14, 4, 7, 8, 11, 0, 3, 12, 15):
        if slot < 4:
            pl.when(has_up)(functools.partial(add, slot, copies[slot]))
        elif slot >= 12:
            pl.when(has_down)(functools.partial(add, slot, copies[slot]))
        else:
            add(slot, copies[slot])

    for copy in small[4:]:
        copy.wait()
    summed = jnp.sum(acc[...] * sens[...].astype(jnp.float32), axis=0, keepdims=True)
    live = lax.broadcasted_iota(jnp.int32, (1, slots), 1) < jnp.broadcast_to(tally[...], (1, slots))
    value = scaled[...] * summed / ((members - 1) * radius_sq * radius_sq)
    out_ref[...] = jnp.where(live, value, 0.0)

    for slot, copy in copies.items():
        if slot < 4:
            pl.when(has_down)(copy.wait_send)
        elif slot >= 12:
            pl.when(has_up)(copy.wait_send)
        else:
            copy.wait_send()


def on_device(nlat, nlon, dev, mis, sens, scaled, loc, cat, codes, tally):
    levels, tile, _, members = dev.shape
    slots = sens.shape[3]
    half = tile // 2
    quad = half * half
    bf16, f32, i32 = jnp.bfloat16, jnp.float32, jnp.int32
    out = pl.pallas_call(
        functools.partial(kernel, nlat, nlon),
        out_shape=jax.ShapeDtypeStruct((1, slots), f32),
        in_specs=[pl.BlockSpec(memory_space=pl.ANY)] * 8,
        out_specs=pl.BlockSpec(memory_space=pltpu.VMEM),
        scratch_shapes=[
            pltpu.VMEM((levels, tile, tile, members), bf16),
            pltpu.VMEM((levels, tile, tile), f32),
            pltpu.VMEM((members, slots), bf16),
            pltpu.VMEM((1, slots), f32),
            pltpu.VMEM((2, slots), i32),
            pltpu.VMEM((1, slots), i32),
            pltpu.VMEM((4, slots), i32),
            pltpu.VMEM((1, 1), i32),
            pltpu.VMEM((2, tile, levels * tile), f32),
            pltpu.VMEM((2, half, half, members), f32),
            pltpu.VMEM((4, members, quad), bf16),
            pltpu.VMEM((16, members, quad), bf16),
            pltpu.VMEM((12, half, slots), bf16),
            pltpu.VMEM((16, half, half, slots), bf16),
            pltpu.VMEM((members, slots), f32),
            pltpu.SemaphoreType.DMA((7,)),
            pltpu.SemaphoreType.DMA((READ_CHUNKS,)),
            pltpu.SemaphoreType.DMA((16,)),
            pltpu.SemaphoreType.DMA((16,)),
        ],
        compiler_params=pltpu.CompilerParams(
            collective_id=0, has_side_effects=True, vmem_limit_bytes=60 * 1024 * 1024
        ),
    )(dev, mis, sens[0, 0], scaled[0], loc[0, 0], cat[0], codes[0, 0], tally)
    return out[None]


def solution(mesh):
    return jax.shard_map(
        functools.partial(on_device, mesh.shape["lat"], mesh.shape["lon"]),
        mesh=mesh,
        in_specs=(
            P(None, "lat", "lon", None),
            P(None, "lat", "lon"),
            P("lat", "lon", None, None),
            P("lat", "lon", None),
            P("lat", "lon", None, None),
            P("lat", "lon", None),
            P("lat", "lon", None, None),
            P("lat", "lon"),
        ),
        out_specs=P("lat", "lon", None),
        check_vma=False,
    )
```

time: 59.5 us -> 18.4 us (0.31)
  the two profiles are of different devices: /device:TPU:0 before, /device:TPU:12 now
where the time goes in v1:
time: 18.4 us; the launch traced here: 18.2 us
  Pallas kernels  16.3 us (89%)
  local copies, waits for them, and re-layouts  1.28 us (7%)
  between operations  0.66 us (4%)
    pallas_call x1, Pallas kernels, on_device(): pl.pallas_call(functools.partial(kernel, nlat, nlon), out_shape=jax.Shape...  16.3 us
    unnamed x1, local copies, waits for them, and re-layouts  1.28 us

profile of v1, /device:TPU:12, one launch (start us, length us, event | category | flops | bytes accessed | tf_op | source)
XLA Modules:
  0.0 18.2 jit_solution(8912603854576621886)
XLA Ops:
  0.7 16.3 %shard_map.82 = f32[1,1024]{1,0:T(1,128)} custom-call(bf16[16,32,32,80]{3,2,1,0:T(8,128)(2,1)} %dev_hbm.1, f32[16,32,32]{2,1,0:T(8,128)} %mis_hbm.1, bf16[80,1024]{1,0:T(8,128)(2,1)} %bitcast.6, f32[1,1024]{1,0:T(1,128)} %bitcast.10, s32[2,1024]{1,0:T(2,128)} %bitcast.9, s32[1,1024]{1,0:T(1,128)} %bitcast.11, s32[4,1024]{1,0:T(4,128)} %bitcast.7, ...), custom_call_target="tpu_custom_call" | custom-call | tf_op jit(solution)/shard_map/pallas_call | solution.py:216
  17.0 1.3 %copy.11 = f32[1,1,1024]{2,1,0:T(1,128)} copy(f32[1,1,1024]{2,1,0:T(1,128)} %bitcast.8) | data formatting | bytes 8192

commit v2 on v1

--- a/solution.py
+++ b/solution.py
@@ -8,7 +8,7 @@
 from jax.sharding import PartitionSpec as P
 
 MESH = pl.DeviceIdType.MESH
-READ_CHUNKS = 4
+HALF_CHUNKS = 2
 
 
 def kernel(
@@ -29,7 +29,11 @@
     has_up = p > 0
     has_down = p < nlat - 1
 
-    rows_per = tile // READ_CHUNKS
+    first = 1 - lax.rem(p, 2)
+    halves = (first, 1 - first)
+    has_first = jnp.where(first == 1, nlat - 1 - p, p) > 0
+    has_second = jnp.where(first == 1, p, nlat - 1 - p) > 0
+    rows_per = half // HALF_CHUNKS
     small = [
         pltpu.make_async_copy(src, dst, in_sem.at[i])
         for i, (src, dst) in enumerate(
@@ -37,14 +41,13 @@
              (sens_hbm, sens), (scaled_hbm, scaled), (tally_hbm, tally)]
         )
     ]
-    reads = [
-        pltpu.make_async_copy(
-            dev_hbm.at[:, pl.ds(c * rows_per, rows_per)],
-            dev.at[:, pl.ds(c * rows_per, rows_per)],
-            dev_sem.at[c],
-        )
-        for c in range(READ_CHUNKS)
-    ]
+    reads = []
+    for yh in halves:
+        for c in range(HALF_CHUNKS):
+            rows = pl.ds(yh * half + c * rows_per, rows_per)
+            reads.append(
+                pltpu.make_async_copy(dev_hbm.at[:, rows], dev.at[:, rows], dev_sem.at[len(reads)])
+            )
     small[0].start()
     reads[0].start()
     for copy in small[1:4]:
@@ -97,31 +100,17 @@
     peers = 2 + 3 * jnp.minimum(p, 1) + 3 * jnp.minimum(nlat - 1 - p, 1)
     pl.semaphore_wait(barrier, peers)
 
-    def send(yh, xh, kind):
-        i = 3 if yh == 0 else 0
-        j = 3 if xh == 0 else 0
-        row = p - 1 if yh == 0 else p + 1
-        col = left if xh == 0 else right
-        if kind == "row":
-            i, row = yh + 1, p
-        if kind == "col":
-            j, col = xh + 1, q
-        slot = i * 4 + j
-        copy = pltpu.make_async_remote_copy(
-            src_ref=own.at[2 * yh + xh],
+    def remote(src, slot, row, col):
+        return pltpu.make_async_remote_copy(
+            src_ref=src,
             dst_ref=halo.at[slot],
             send_sem=send_sem.at[slot],
             recv_sem=recv_sem.at[slot],
             device_id=(row, col),
             device_id_type=MESH,
         )
-        return slot, copy, kind != "row"
-
-    copies = {}
-    for yh in range(2):
-        for c in range(yh * READ_CHUNKS // 2, (yh + 1) * READ_CHUNKS // 2):
-            reads[c].wait()
-
+
+    for stage, yh in enumerate(halves):
         def level_sum(y, _):
             row = yh * half + y
             terms = []
@@ -140,16 +129,36 @@
             cells[1, y] = total[half:]
             return 0
 
-        lax.fori_loop(0, half, level_sum, 0, unroll=4)
+        for c in range(HALF_CHUNKS):
+            reads[stage * HALF_CHUNKS + c].wait()
+            lax.fori_loop(c * rows_per, (c + 1) * rows_per, level_sum, 0, unroll=True)
+        beyond = p + 2 * yh - 1
+        edge = 12 * (1 - yh)
         for xh in range(2):
-            own[2 * yh + xh] = cells[xh].reshape(half * half, members).T.astype(jnp.bfloat16)
-            for kind in ("row", "corner", "col"):
-                slot, copy, vertical = send(yh, xh, kind)
-                copies[slot] = copy
-                if vertical:
-                    pl.when(has_up if yh == 0 else has_down)(copy.start)
-                else:
-                    copy.start()
+            j, col = (3, left) if xh == 0 else (0, right)
+            mine = 2 * yh + xh
+            own[mine] = cells[xh].reshape(half * half, members).T.astype(jnp.bfloat16)
+            source = own.at[mine]
+            remote(source, 4 * (yh + 1) + j, p, col).start()
+            if stage == 0:
+                pl.when(has_first)(remote(source, edge + xh + 1, beyond, q).start)
+            else:
+                @pl.when(has_second)
+                def _():
+                    remote(source, edge + j, beyond, col).start()
+                    remote(source, edge + xh + 1, beyond, q).start()
+
+    def relay(j):
+        slot = 4 * (first + 1) + j
+        remote(halo.at[slot], slot, p, right).wait_recv()
+        copy = remote(halo.at[slot], 12 * (1 - first) + j, p + 2 * first - 1, q)
+        pl.when(has_first)(copy.start)
+
+    near = 3 * (1 - jnp.minimum(q, 1))
+    copies = {
+        slot: remote(own.at[0], slot, p, right)
+        for slot in (1, 2, 13, 14, 4, 7, 8, 11, 0, 3, 12, 15)
+    }
 
     row_gap = jnp.broadcast_to(place[0:1], (half, slots)).astype(jnp.bfloat16)
     reach = jnp.broadcast_to(radius_sq, (half, slots)).astype(jnp.bfloat16)
@@ -172,10 +181,14 @@
             preferred_element_type=jnp.float32,
         )
 
-    def add(slot, copy):
-        copy.wait_recv()
+    def add(slot):
         acc[...] += product(slot, halo[slot])
 
+    def receive(slot):
+        copies[slot].wait_recv()
+        add(slot)
+
+    relay(near)
     for yh in range(2):
         for xh in range(2):
             value = product((yh + 1) * 4 + xh + 1, own[2 * yh + xh])
@@ -183,13 +196,15 @@
                 acc[...] = value
             else:
                 acc[...] += value
-    for slot in (1, 2, 13, 14, 4, 7, 8, 11, 0, 3, 12, 15):
-        if slot < 4:
-            pl.when(has_up)(functools.partial(add, slot, copies[slot]))
-        elif slot >= 12:
-            pl.when(has_down)(functools.partial(add, slot, copies[slot]))
-        else:
-            add(slot, copies[slot])
+    for slot in (1, 2, 13, 14):
+        pl.when(has_up if slot < 4 else has_down)(functools.partial(receive, slot))
+    relay(3 - near)
+    for yh in range(2):
+        for slot in (4 * yh + 4, 4 * yh + 7):
+            pl.when(first != yh)(copies[slot].wait_recv)
+            add(slot)
+    for slot in (0, 3, 12, 15):
+        pl.when(has_up if slot < 4 else has_down)(functools.partial(receive, slot))
 
     for copy in small[4:]:
         copy.wait()
@@ -235,7 +250,7 @@
             pltpu.VMEM((16, half, half, slots), bf16),
             pltpu.VMEM((members, slots), f32),
             pltpu.SemaphoreType.DMA((7,)),
-            pltpu.SemaphoreType.DMA((READ_CHUNKS,)),
+            pltpu.SemaphoreType.DMA((2 * HALF_CHUNKS,)),
             pltpu.SemaphoreType.DMA((16,)),
             pltpu.SemaphoreType.DMA((16,)),
         ],

time: 18.4 us -> 17.3 us (0.940)
  the two profiles are of different devices: /device:TPU:12 before, /device:TPU:1 now
where the time goes in v2:
time: 17.3 us; the launch traced here: 17.1 us
  Pallas kernels  15.2 us (88%)
  local copies, waits for them, and re-layouts  1.28 us (7%)
  between operations  0.66 us (4%)
    pallas_call x1, Pallas kernels, on_device(): pl.pallas_call(functools.partial(kernel, nlat, nlon), out_shape=jax.Shape...  15.2 us
    unnamed x1, local copies, waits for them, and re-layouts  1.28 us

profile of v2, /device:TPU:1, one launch (start us, length us, event | category | flops | bytes accessed | tf_op | source)
XLA Modules:
  0.0 17.1 jit_solution(5988314162780318290)
XLA Ops:
  0.7 15.2 %shard_map.82 = f32[1,1024]{1,0:T(1,128)} custom-call(bf16[16,32,32,80]{3,2,1,0:T(8,128)(2,1)} %dev_hbm.1, f32[16,32,32]{2,1,0:T(8,128)} %mis_hbm.1, bf16[80,1024]{1,0:T(8,128)(2,1)} %bitcast.6, f32[1,1024]{1,0:T(1,128)} %bitcast.10, s32[2,1024]{1,0:T(2,128)} %bitcast.9, s32[1,1024]{1,0:T(1,128)} %bitcast.11, s32[4,1024]{1,0:T(4,128)} %bitcast.7, ...), custom_call_target="tpu_custom_call" | custom-call | tf_op jit(solution)/shard_map/pallas_call | solution.py:231
  15.9 1.3 %copy.11 = f32[1,1,1024]{2,1,0:T(1,128)} copy(f32[1,1,1024]{2,1,0:T(1,128)} %bitcast.8) | data formatting | bytes 8192

commit v3 on v2

--- a/solution.py
+++ b/solution.py
@@ -29,10 +29,9 @@
     has_up = p > 0
     has_down = p < nlat - 1
 
-    first = 1 - lax.rem(p, 2)
+    first = lax.rem(p, 2)
     halves = (first, 1 - first)
-    has_first = jnp.where(first == 1, nlat - 1 - p, p) > 0
-    has_second = jnp.where(first == 1, p, nlat - 1 - p) > 0
+    present = [jnp.where(yh == 1, nlat - 1 - p, p) > 0 for yh in halves]
     rows_per = half // HALF_CHUNKS
     small = [
         pltpu.make_async_copy(src, dst, in_sem.at[i])
@@ -97,9 +96,6 @@
         == lax.broadcasted_iota(jnp.int32, (tile, levels * tile), 0)
     )
 
-    peers = 2 + 3 * jnp.minimum(p, 1) + 3 * jnp.minimum(nlat - 1 - p, 1)
-    pl.semaphore_wait(barrier, peers)
-
     def remote(src, slot, row, col):
         return pltpu.make_async_remote_copy(
             src_ref=src,
@@ -132,27 +128,26 @@
         for c in range(HALF_CHUNKS):
             reads[stage * HALF_CHUNKS + c].wait()
             lax.fori_loop(c * rows_per, (c + 1) * rows_per, level_sum, 0, unroll=True)
+        for xh in range(2):
+            own[2 * yh + xh] = cells[xh].reshape(half * half, members).T.astype(jnp.bfloat16)
+        if stage == 0:
+            peers = 2 + 3 * jnp.minimum(p, 1) + 3 * jnp.minimum(nlat - 1 - p, 1)
+            pl.semaphore_wait(barrier, peers)
         beyond = p + 2 * yh - 1
         edge = 12 * (1 - yh)
         for xh in range(2):
             j, col = (3, left) if xh == 0 else (0, right)
             mine = 2 * yh + xh
-            own[mine] = cells[xh].reshape(half * half, members).T.astype(jnp.bfloat16)
             source = own.at[mine]
             remote(source, 4 * (yh + 1) + j, p, col).start()
-            if stage == 0:
-                pl.when(has_first)(remote(source, edge + xh + 1, beyond, q).start)
-            else:
-                @pl.when(has_second)
-                def _():
-                    remote(source, edge + j, beyond, col).start()
-                    remote(source, edge + xh + 1, beyond, q).start()
-
-    def relay(j):
-        slot = 4 * (first + 1) + j
+            pl.when(present[stage])(remote(source, edge + xh + 1, beyond, q).start)
+
+    def relay(stage, j):
+        yh = halves[stage]
+        slot = 4 * (yh + 1) + j
         remote(halo.at[slot], slot, p, right).wait_recv()
-        copy = remote(halo.at[slot], 12 * (1 - first) + j, p + 2 * first - 1, q)
-        pl.when(has_first)(copy.start)
+        copy = remote(halo.at[slot], 12 * (1 - yh) + j, p + 2 * yh - 1, q)
+        pl.when(present[stage])(copy.start)
 
     near = 3 * (1 - jnp.minimum(q, 1))
     copies = {
@@ -188,7 +183,7 @@
         copies[slot].wait_recv()
         add(slot)
 
-    relay(near)
+    relay(0, near)
     for yh in range(2):
         for xh in range(2):
             value = product((yh + 1) * 4 + xh + 1, own[2 * yh + xh])
@@ -198,10 +193,11 @@
                 acc[...] += value
     for slot in (1, 2, 13, 14):
         pl.when(has_up if slot < 4 else has_down)(functools.partial(receive, slot))
-    relay(3 - near)
+    relay(1, near)
+    relay(0, 3 - near)
+    relay(1, 3 - near)
     for yh in range(2):
         for slot in (4 * yh + 4, 4 * yh + 7):
-            pl.when(first != yh)(copies[slot].wait_recv)
             add(slot)
     for slot in (0, 3, 12, 15):
         pl.when(has_up if slot < 4 else has_down)(functools.partial(receive, slot))

time: 17.3 us -> 16.9 us (0.977)
  Pallas kernels: 15.2 us -> 14.7 us
    pallas_call x1, Pallas kernels: 15.2 us -> 14.7 us  [on_device(): pl.pallas_call(functools.partial(kernel, nlat, nlon), out_shape=jax.Shape...]
where the time goes in v3:
time: 16.9 us; the launch traced here: 16.7 us
  Pallas kernels  14.7 us (87%)
  local copies, waits for them, and re-layouts  1.28 us (8%)
  between operations  0.66 us (4%)
    pallas_call x1, Pallas kernels, on_device(): pl.pallas_call(functools.partial(kernel, nlat, nlon), out_shape=jax.Shape...  14.7 us
    unnamed x1, local copies, waits for them, and re-layouts  1.28 us

profile of v3, /device:TPU:1, one launch (start us, length us, event | category | flops | bytes accessed | tf_op | source)
XLA Modules:
  0.0 16.7 jit_solution(8629024679331491817)
XLA Ops:
  0.7 14.7 %shard_map.82 = f32[1,1024]{1,0:T(1,128)} custom-call(bf16[16,32,32,80]{3,2,1,0:T(8,128)(2,1)} %dev_hbm.1, f32[16,32,32]{2,1,0:T(8,128)} %mis_hbm.1, bf16[80,1024]{1,0:T(8,128)(2,1)} %bitcast.6, f32[1,1024]{1,0:T(1,128)} %bitcast.10, s32[2,1024]{1,0:T(2,128)} %bitcast.9, s32[1,1024]{1,0:T(1,128)} %bitcast.11, s32[4,1024]{1,0:T(4,128)} %bitcast.7, ...), custom_call_target="tpu_custom_call" | custom-call | tf_op jit(solution)/shard_map/pallas_call | solution.py:227
  15.4 1.3 %copy.11 = f32[1,1,1024]{2,1,0:T(1,128)} copy(f32[1,1,1024]{2,1,0:T(1,128)} %bitcast.8) | data formatting | bytes 8192
